TPU v7x, 32 devices: a whole 2x2x4 slice. The times are simulated.
32 devices in a mesh: client: 4 (over x, core), blk: 8 (over z, y).
Axes of the slice: x: 2, y: 2, z: 4, core: 2. Of those that a mesh axis runs over, the one named last changes fastest.
Arguments:
- activations: bfloat16 [8, 2, 8, 8, 1280], P('client', None, 'blk'), may hold values from -6 to 6
- sample_count: int32 [8], replicated, may hold values from 1 to 2, as said below
- client_weights: bfloat16 [8, 11520, 1280], P('client', 'blk'), may hold values from -6 to 6
Outputs:
- merged_gram: float32 [11520, 11520], P(('blk', 'client'))
- merged_rhs: float32 [11520, 1280], P(('blk', 'client'))
Inputs may be any that keep to these rules, and one draw needn't show every extreme that they name: `sample_count`: some client has all 2 slots live in every draw.
All inputs are finite; a program needn't handle non-finite values.
Results may differ from a plain program's by a relative error of at most 0.0029.
Values may be sent and summed in bfloat16 or wider, within the bound.
A program may use at most 192 MiB of HBM per device.

v0:
```python
import functools

import jax
import jax.numpy as jnp
from jax import lax
from jax.experimental import pallas as pl
from jax.experimental.pallas import tpu as pltpu
from jax.sharding import PartitionSpec as P

keep_off = 0.9
LANES = 128


MESH = pl.DeviceIdType.MESH


def pixel_rows(count_ref, base, pixels, groups, slots, height, stride, width):
    lane = lax.broadcasted_iota(jnp.int32, (1, pixels), 1)
    slot = (lane // width) % slots
    client = (lane // (height * stride)) * groups + (lane // (slots * width)) % groups
    count = jnp.zeros((1, pixels), jnp.int32)
    for index in range(pixels // (height * slots * width)):
        count = jnp.where(client == index, count_ref[base + index], count)
    live = jnp.where(slot < count, 1.0, 0.0)
    total = count_ref.shape[0] * height * width
    return live, 1.0 / (total * count.astype(jnp.float32))


def expand(base_of, live, channels, scratch, height, stride, width):
    pixels = live.shape[1]
    lane = lax.broadcasted_iota(jnp.int32, (1, pixels), 1)
    col = lane % width
    row = (lane // stride) % height

    def shifted(value, step, inside):
        return jnp.where(inside, pltpu.roll(value, (-step) % pixels, 1), 0.0)

    for first in range(0, channels, 16):
        size = min(16, channels - first)
        base = jnp.where(live > 0.0, base_of(first, size), 0.0)
        for b in range(3):
            if b == 1:
                across = base
            else:
                across = shifted(base, b - 1, (col + (b - 1) >= 0) & (col + (b - 1) < width))
            for a in range(3):
                if a == 1:
                    both = across
                else:
                    both = shifted(across, (a - 1) * stride, (row + (a - 1) >= 0) & (row + (a - 1) < height))
                for chunk in range(pixels // LANES):
                    scratch[chunk, pl.ds(first * 9 + 3 * a + b, size, stride=9), :] = both[
                        :, chunk * LANES : (chunk + 1) * LANES
                    ]


def gather_kernel(x_ref, out_ref, recv_sem, send_sem):
    clients, blks = out_ref.shape[:2]
    rows = out_ref.shape[2]
    depth = blks // 2
    client, blk = lax.axis_index("client"), lax.axis_index("blk")
    core_mate = client + 1 - 2 * (client % 2)
    x_mate = (client + 2) % clients
    z, y = blk // 2, blk % 2
    y_mate = blk + 1 - 2 * y
    core_dev, x_dev, y_dev = (core_mate, blk), (x_mate, blk), (client, y_mate)
    up_dev, down_dev = (client, blk + 2), (client, blk - 2)
    half = rows // 2

    barrier = pltpu.get_barrier_semaphore()
    for device in (core_dev, x_dev, y_dev):
        pl.semaphore_signal(barrier, inc=1, device_id=device, device_id_type=MESH)

    @pl.when(z + 1 < depth)
    def _():
        pl.semaphore_signal(barrier, inc=1, device_id=up_dev, device_id_type=MESH)

    @pl.when(z > 0)
    def _():
        pl.semaphore_signal(barrier, inc=1, device_id=down_dev, device_id_type=MESH)

    pl.semaphore_wait(barrier, 3 + jnp.where(z > 0, 1, 0) + jnp.where(z + 1 < depth, 1, 0))

    def copy(lane, c, b, device, part=None, own=False):
        where = (c, b) if part is None else (c, b, pl.ds(part * half, half))
        dst = out_ref.at[where]
        src = dst
        if own:
            src = x_ref
        if part is None:
            recv = recv_sem.at[0, c * blks + b]
        else:
            recv = recv_sem.at[part, c * blks + b]
        return pltpu.make_async_remote_copy(
            src_ref=src,
            dst_ref=dst,
            send_sem=send_sem.at[lane, c * blks + b],
            recv_sem=recv,
            device_id=device,
            device_id_type=MESH,
        )

    def along_z(offset):
        if offset == 0:
            return None
        level = z + offset
        return (level >= 0) & (level < depth)

    def guarded(offset, action):
        inside = along_z(offset)
        if inside is None:
            action(blk)
        else:
            pl.when(inside)(lambda: action(blk + 2 * offset))

    order = [0]
    for distance in range(1, depth):
        order += [-distance, distance]

    for offset in order:

        def first(b):
            own = offset == 0
            if not own:
                copy(0, client, b, core_dev).wait_recv()
            if offset <= 0:

                @pl.when(z + 1 < depth)
                def _():
                    copy(0, client, b, up_dev, own=own).start()

            if offset >= 0:

                @pl.when(z > 0)
                def _():
                    copy(1, client, b, down_dev, own=own).start()

            copy(2, client, b, x_dev, own=own).start()
            copy(3, client, b, y_dev, own=own).start()
            copy(4, client, b, core_dev, own=own).start()

        guarded(offset, first)

    def mate_of(b):
        return b + 1 - 2 * y

    for offset in order:

        def second(b):
            copy(0, x_mate, b, core_dev).wait_recv()
            copy(3, x_mate, b, y_dev, part=0).start()
            copy(4, x_mate, b, core_dev).start()
            copy(0, client, mate_of(b), core_dev).wait_recv()
            copy(2, client, mate_of(b), x_dev, part=1).start()
            copy(4, client, mate_of(b), core_dev).start()

        guarded(offset, second)

    for offset in order:

        def third(b):
            copy(0, x_mate, mate_of(b), core_dev, part=0).wait_recv()
            copy(0, x_mate, mate_of(b), core_dev, part=1).wait_recv()
            copy(4, x_mate, mate_of(b), core_dev).start()

        guarded(offset, third)

    for offset in order:

        def fourth(b):
            far = (core_mate + 2) % clients
            for c, bb in ((core_mate, b), (far, b), (core_mate, mate_of(b)), (far, mate_of(b))):
                copy(0, c, bb, core_dev).wait_recv()
            own = offset == 0
            if offset <= 0:

                @pl.when(z + 1 < depth)
                def _():
                    copy(0, client, b, up_dev, own=own).wait_send()

            if offset >= 0:

                @pl.when(z > 0)
                def _():
                    copy(1, client, b, down_dev, own=own).wait_send()

            copy(2, client, b, x_dev, own=own).wait_send()
            copy(3, client, b, y_dev, own=own).wait_send()
            copy(4, client, b, core_dev, own=own).wait_send()
            copy(3, x_mate, b, y_dev, part=0).wait_send()
            copy(4, x_mate, b, core_dev).wait_send()
            copy(2, client, mate_of(b), x_dev, part=1).wait_send()
            copy(4, client, mate_of(b), core_dev).wait_send()
            copy(4, x_mate, mate_of(b), core_dev).wait_send()

        guarded(offset, fourth)

    out_ref[client, blk] = x_ref[...]


def gather_call(x, clients, blks):
    return pl.pallas_call(
        gather_kernel,
        in_specs=[pl.BlockSpec(memory_space=pltpu.VMEM)],
        out_specs=pl.BlockSpec(memory_space=pltpu.VMEM),
        out_shape=jax.ShapeDtypeStruct((clients, blks) + x.shape, x.dtype),
        scratch_shapes=[
            pltpu.SemaphoreType.DMA((2, clients * blks)),
            pltpu.SemaphoreType.DMA((5, clients * blks)),
        ],
        compiler_params=pltpu.CompilerParams(
            collective_id=1, has_side_effects=True, vmem_limit_bytes=40 * 1024 * 1024
        ),
    )(x)


def rhs_kernel(
    height, stride, width, groups, slots, count_ref, x_ref, w_ref, keep_ref, away_ref,
    wbuf, wide, patch, scaled, square, part_ref, ybuf, sums, zbuf, obuf, rbuf, abuf, cbuf,
    ws, ys, yr, zs, zr, gs, gr, fs, fr, cs, cr,
):
    pieces, depth = part_ref.shape[:2]
    cols = part_ref.shape[4]
    pixels = x_ref.shape[1]
    tall = wide.shape[1]
    client, blk = lax.axis_index("client"), lax.axis_index("blk")
    z, y = blk // 2, blk % 2
    core, side = client % 2, client // 2
    other = 1 - y
    y_dev = (client, blk + 1 - 2 * y)
    core_dev = (client + 1 - 2 * core, blk)
    mine = keep_ref.shape[0]

    def level(d):
        return (z + d) % depth

    def z_dev(d):
        return (client, level(d) * 2 + y)

    def w_copy(q):
        return pltpu.make_async_copy(w_ref.at[:, :, pl.ds(q * cols, cols)], wbuf.at[q], ws.at[q])

    for q in range(pieces):
        w_copy(q).start()

    barrier = pltpu.get_barrier_semaphore()
    pl.semaphore_signal(barrier, inc=1, device_id=y_dev, device_id_type=MESH)
    pl.semaphore_signal(barrier, inc=1, device_id=core_dev, device_id_type=MESH)
    for d in range(1, depth):
        pl.semaphore_signal(barrier, inc=1, device_id=z_dev(d), device_id_type=MESH)

    live, scale = pixel_rows(count_ref, client * groups, pixels, groups, slots, height, stride, width)
    who = (lax.broadcasted_iota(jnp.int32, (1, pixels), 1) // (slots * width)) % groups
    expand(
        lambda first, size: x_ref[first : first + size, :].astype(jnp.float32),
        live, x_ref.shape[0], wide, height, stride, width,
    )
    for chunk in range(wide.shape[0]):
        span = slice(chunk * LANES, (chunk + 1) * LANES)
        value = wide[chunk]
        patch[:, span] = value.astype(jnp.bfloat16)
        scaled[:, span] = (value * scale[:, span]).astype(jnp.bfloat16)
    pl.semaphore_wait(barrier, depth + 1)

    def send(src, dst, send_sem, recv_sem, device):
        return pltpu.make_async_remote_copy(
            src_ref=src, dst_ref=dst, send_sem=send_sem, recv_sem=recv_sem, device_id=device, device_id_type=MESH
        )

    def y_copy(q):
        return send(part_ref.at[q, :, other], ybuf.at[q], ys.at[q], yr.at[q], y_dev)

    def z_copy(q, d):
        return send(sums.at[q, level(d)], zbuf.at[q, d], zs.at[q, d], zr.at[q, d], z_dev(d))

    def share(q, d, to):
        here = obuf.at[q, level(d), y]
        return send(here, here, gs.at[q, to], gr.at[q, to], z_dev(to))

    def forward(q, d, column):
        here = obuf.at[q, level(d), column]
        return send(here, here, fs.at[q, d], fr.at[q, level(d)], y_dev)

    def core_copy(q):
        return send(abuf.at[q], cbuf.at[q], cs.at[q], cr.at[q], core_dev)

    def multiply(q):
        w_copy(q).wait()
        total = None
        for group in range(groups):
            picked = jnp.where(who == group, patch[...].astype(jnp.float32), 0.0).astype(jnp.bfloat16)
            term = lax.dot_general(
                picked, wbuf[q, group], (((0,), (0,)), ((), ())), preferred_element_type=jnp.float32
            )
            total = term if total is None else total + term
        part_ref[q] = total.reshape(part_ref.shape[1:])
        y_copy(q).start()

    def damping():
        for group in range(groups):
            term = jnp.zeros((tall, 1), jnp.float32)
            for chunk in range(wide.shape[0]):
                span = slice(chunk * LANES, (chunk + 1) * LANES)
                value = wide[chunk]
                value = jnp.where(who[:, span] == group, value * value * scale[:, span], 0.0)
                term += jnp.sum(value, axis=1, keepdims=True)
            square[group] = term * (1.0 - keep_off)

    def damp(q):
        total = None
        for group in range(groups):
            term = square[group] * wbuf[q, group].astype(jnp.float32)
            total = term if total is None else total + term
        rbuf[q] = total

    def add_y(q):
        y_copy(q).wait_recv()
        for d in range(depth):
            sums[q, level(d)] = part_ref[q, level(d), y] + ybuf[q, level(d)]
        for d in range(1, depth):
            z_copy(q, d).start()

    def add_z(q):
        total = sums[q, z]
        for d in range(1, depth):
            z_copy(q, d).wait_recv()
            total = total + zbuf[q, d]
        obuf[q, z, y] = total.astype(jnp.bfloat16)
        for d in range(1, depth):
            share(q, 0, d).start()
        forward(q, 0, y).start()

    def pass_on(q):
        for d in range(1, depth):
            share(q, depth - d, d).wait_recv()
            forward(q, depth - d, y).start()

    def rows_of(q, holder):
        if mine % 8 == 0:
            return rbuf[q, pl.ds(pl.multiple_of(holder * mine, 8), mine), :]
        value = rbuf[q, :mine, :]
        for index in range(1, tall // mine):
            value = jnp.where(holder == index, rbuf[q, index * mine : (index + 1) * mine, :], value)
        return value

    def cross(q):
        for d in range(depth):
            forward(q, d, other).wait_recv()
        product = jnp.dot(scaled[...], obuf[q].reshape(pixels, cols), preferred_element_type=jnp.float32)
        rbuf[q] = rbuf[q] + keep_off * product
        for far in range(2):
            abuf[q, far] = rows_of(q, far * 2 + 1 - core).astype(jnp.bfloat16)
        core_copy(q).start()

    def finish(q):
        core_copy(q).wait_recv()
        span = slice(q * cols, (q + 1) * cols)
        keep_ref[:, span] = rows_of(q, client) + cbuf[q, side].astype(jnp.float32)
        far = 1 - side
        away = rows_of(q, far * 2 + core) + cbuf[q, far].astype(jnp.float32)
        away_ref[:, span] = away.astype(jnp.bfloat16)

    for q in range(pieces):
        multiply(q)
    damping()
    for step in range(pieces + 4):
        if step < pieces:
            add_y(step)
        if 0 <= step - 1 < pieces:
            add_z(step - 1)
        if step < pieces:
            damp(step)
        if 0 <= step - 2 < pieces:
            pass_on(step - 2)
        if 0 <= step - 3 < pieces:
            cross(step - 3)
        if 0 <= step - 4 < pieces:
            finish(step - 4)

    for q in range(pieces):
        y_copy(q).wait_send()
        core_copy(q).wait_send()
        for d in range(1, depth):
            z_copy(q, d).wait_send()
            share(q, 0, d).wait_send()
        for d in range(depth):
            forward(q, d, y).wait_send()


def rhs_call(counts, x, weights, blks, mine, slots, height, stride, width):
    channels, pixels = x.shape
    groups, tall, columns = weights.shape
    pieces = columns // 256 if columns % 256 == 0 else 1
    cols = columns // pieces
    depth = blks // 2
    rows = pixels // blks
    sem = pltpu.SemaphoreType.DMA
    hop = pltpu.VMEM((pieces, depth, rows, cols), jnp.float32)
    return pl.pallas_call(
        functools.partial(rhs_kernel, height, stride, width, groups, slots),
        in_specs=[
            pl.BlockSpec(memory_space=pltpu.SMEM),
            pl.BlockSpec(memory_space=pltpu.VMEM),
            pl.BlockSpec(memory_space=pl.ANY),
        ],
        out_specs=[pl.BlockSpec(memory_space=pltpu.VMEM)] * 2,
        out_shape=[
            jax.ShapeDtypeStruct((mine, columns), jnp.float32),
            jax.ShapeDtypeStruct((mine, columns), jnp.bfloat16),
        ],
        scratch_shapes=[
            pltpu.VMEM((pieces, groups, tall, cols), jnp.bfloat16),
            pltpu.VMEM((pixels // LANES, tall, LANES), jnp.float32),
            pltpu.VMEM((tall, pixels), jnp.bfloat16),
            pltpu.VMEM((tall, pixels), jnp.bfloat16),
            pltpu.VMEM((groups, tall, 1), jnp.float32),
            pltpu.VMEM((pieces, depth, 2, rows, cols), jnp.float32),
            hop,
            hop,
            hop,
            pltpu.VMEM((pieces, depth, 2, rows, cols), jnp.bfloat16),
            pltpu.VMEM((pieces, tall, cols), jnp.float32),
            pltpu.VMEM((pieces, 2, mine, cols), jnp.bfloat16),
            pltpu.VMEM((pieces, 2, mine, cols), jnp.bfloat16),
            sem((pieces,)),
            sem((pieces,)),
            sem((pieces,)),
        ]
        + [sem((pieces, depth))] * 6
        + [sem((pieces,))] * 2,
        compiler_params=pltpu.CompilerParams(
            collective_id=2, has_side_effects=True, vmem_limit_bytes=60 * 1024 * 1024
        ),
    )(counts, x, weights)


def gram_kernel(height, stride, width, groups, slots, first_ref, count_ref, x_ref, own_ref, gram_ref, wide, narrow, mine_wide, mine_ref, flipped):
    step = pl.program_id(0)
    chunks = wide.shape[0]

    live, scale = pixel_rows(count_ref, 0, x_ref.shape[0], groups, slots, height, stride, width)

    @pl.when(step == 0)
    def _():
        expand(
            lambda first, size: own_ref[first : first + size, :].astype(jnp.float32),
            live, own_ref.shape[0], mine_wide, height, stride, width,
        )
        for chunk in range(chunks):
            part = slice(chunk * LANES, (chunk + 1) * LANES)
            mine_ref[:, part] = (mine_wide[chunk] * scale[:, part]).astype(jnp.bfloat16)

    flipped[...] = x_ref[...].astype(jnp.float32).T
    expand(
        lambda first, size: flipped[first : first + size, :],
        live, flipped.shape[0], wide, height, stride, width,
    )
    for chunk in range(chunks):
        narrow[:, chunk * LANES : (chunk + 1) * LANES] = wide[chunk].astype(jnp.bfloat16)
    product = lax.dot_general(
        mine_ref[...], narrow[...], (((1,), (1,)), ((), ())), preferred_element_type=jnp.float32
    )
    where_diag = first_ref[0] - step * product.shape[1]
    on_diag = (
        lax.broadcasted_iota(jnp.int32, product.shape, 1)
        == lax.broadcasted_iota(jnp.int32, product.shape, 0) + where_diag
    )
    gram_ref[...] = jnp.where(on_diag, product, keep_off * product)


def gram_call(first_row, counts, x, own, groups, slots, height, stride, width):
    pixels, channels = x.shape
    mine = own.shape[0]
    tile = LANES
    return pl.pallas_call(
        functools.partial(gram_kernel, height, stride, width, groups, slots),
        grid=(channels // tile,),
        in_specs=[
            pl.BlockSpec(memory_space=pltpu.SMEM),
            pl.BlockSpec(memory_space=pltpu.SMEM),
            pl.BlockSpec((pixels, tile), lambda j: (0, j)),
            pl.BlockSpec((mine, pixels), lambda j: (0, 0)),
        ],
        out_specs=pl.BlockSpec((mine * 9, tile * 9), lambda j: (0, j)),
        out_shape=jax.ShapeDtypeStruct((mine * 9, channels * 9), jnp.float32),
        scratch_shapes=[
            pltpu.VMEM((pixels // LANES, tile * 9, LANES), jnp.float32),
            pltpu.VMEM((tile * 9, pixels), jnp.bfloat16),
            pltpu.VMEM((pixels // LANES, mine * 9, LANES), jnp.float32),
            pltpu.VMEM((mine * 9, pixels), jnp.bfloat16),
            pltpu.VMEM((tile, pixels), jnp.float32),
        ],
        compiler_params=pltpu.CompilerParams(vmem_limit_bytes=60 * 1024 * 1024),
        cost_estimate=pl.CostEstimate(
            flops=2 * mine * 9 * channels * 9 * pixels,
            bytes_accessed=mine * channels * 81 * 4,
            transcendentals=0,
        ),
    )(first_row, counts, x, own)


def body(activations, sample_count, client_weights):
    blk_count = lax.axis_size("blk")
    client_here = lax.axis_index("client")
    blk_here = lax.axis_index("blk")
    group_size, slot_count, rows_here, width, channels = activations.shape
    height = rows_here * blk_count
    client_groups = sample_count.shape[0] // group_size
    stride = group_size * slot_count * width
    group_pixels = height * stride

    shard = activations.transpose(2, 0, 1, 3, 4).reshape(rows_here * stride, channels)
    gathered = gather_call(shard, client_groups, blk_count).reshape(client_groups * group_pixels, channels)

    tile = channels // blk_count
    mine = tile // client_groups
    first = blk_here * tile
    own = first + client_here * mine
    own_x = lax.dynamic_slice_in_dim(gathered, own, mine, 1).T
    group_x = lax.dynamic_slice(gathered, (client_here * group_pixels, first), (group_pixels, tile)).T
    keep, away = rhs_call(
        sample_count, group_x, client_weights, blk_count, mine * 9, slot_count, height, stride, width
    )
    back = lax.ppermute(away, "client", [(c, (c + 2) % client_groups) for c in range(client_groups)])
    gram = gram_call(
        (own * 9).astype(jnp.int32)[None], sample_count, gathered, own_x,
        group_size, slot_count, height, stride, width,
    )
    return gram, keep + back.astype(jnp.float32)


def solution(mesh):
    in_specs = (P("client", None, "blk", None, None), P(), P("client", "blk", None))
    out_specs = (P(("blk", "client"), None), P(("blk", "client"), None))
    return jax.shard_map(body, mesh=mesh, in_specs=in_specs, out_specs=out_specs, check_vma=False)
```

profile of v0, /device:TPU:0, one launch (start us, length us, event | category | flops | bytes accessed | tf_op | source)
XLA Modules:
  0.0 102.1 jit_solution(16134145527862334445)
XLA Ops:
  0.6 0.0 copy-start.1
  0.6 0.9 copy-done.1
  1.5 24.9 %shard_map.50 = bf16[4,8,32,1280]{3,2,1,0:T(8,128)(2,1)S(1)} custom-call(bf16[32,1280]{1,0:T(8,128)(2,1)S(1)} %bitcast.8), custom_call_target="tpu_custom_call" | custom-call | tf_op jit(solution)/shard_map/pallas_call | solution.py:202
  26.4 0.0 copy-start
  26.4 0.1 dynamic_slice.7
  26.6 1.0 copy.10
  27.6 41.9 %shard_map.52 = (f32[360,1280]{1,0:T(8,128)}, bf16[360,1280]{1,0:T(8,128)(2,1)}) custom-call(s32[8]{0:T(128)} %count_ref.3, bf16[160,256]{1,0:T(8,128)(2,1)} %bitcast.9, bf16[2,1440,1280]{2,1,0:T(8,128)(2,1)} %w_ref.1), custom_call_target="tpu_custom_call" | custom-call | tf_op jit(solution)/shard_map/pallas_call | solution.py:399
  69.4 1.2 %collective-permute-start = (bf16[360,1280]{1,0:T(8,128)(2,1)}, bf16[360,1280]{1,0:T(8,128)(2,1)}, u32[]{:S(2)}, u32[]{:S(2)}) collective-permute-start(bf16[360,1280]{1,0:T(8,128)(2,1)} %get-tuple-element.5), channel_id=1, source_target_pairs={{0,16},{8,24},{16,0},{24,8},{1,17},{9,25},{17,1},{25,9},{2,18},{10... | collective-permute-start | bytes 2764808 | tf_op jit(solution)/shard_map/ppermute | solution.py:524
  70.6 0.0 copy-done
  70.6 0.1 constant_dynamic-slice_fusion
  70.8 0.8 copy.9
  71.5 0.0 copy-start.2
  71.5 28.0 %shard_map.51 = f32[360,11520]{1,0:T(8,128)} custom-call(s32[1]{0:T(128)} %bitcast.first_ref, s32[8]{0:T(128)} %count_ref.3, bf16[1024,1280]{1,0:T(8,128)(2,1)} %bitcast.7, bf16[40,1024]{1,0:T(8,128)(2,1)} %bitcast.10), custom_call_target="tpu_custom_call" | custom-call | flops 8493465600 | bytes 16588800 | tf_op jit(solution)/shard_map/pallas_call | solution.py:475
  99.5 0.0 collective-permute-done
  99.5 0.0 copy-done.2
  99.5 2.6 %convert_add_fusion = f32[360,1280]{1,0:T(8,128)} fusion(f32[360,1280]{1,0:T(8,128)S(1)} %copy-done.2, bf16[360,1280]{1,0:T(8,128)(2,1)} %collective-permute-done), kind=kLoop, calls=%fused_computation | loop fusion | flops 921600 | bytes 4608000 | tf_op jit(solution)/shard_map/add | solution.py:529
Async XLA Ops:
  0.6 0.9 copy-start.1
  26.4 44.2 %copy-start = (bf16[4,8,32,1280]{3,2,1,0:T(8,128)(2,1)}, bf16[4,8,32,1280]{3,2,1,0:T(8,128)(2,1)S(1)}, u32[]{:S(2)}) copy-start(bf16[4,8,32,1280]{3,2,1,0:T(8,128)(2,1)S(1)} %shard_map.50) | copy-start | bytes 7864324
  69.4 30.1 %collective-permute-start = (bf16[360,1280]{1,0:T(8,128)(2,1)}, bf16[360,1280]{1,0:T(8,128)(2,1)}, u32[]{:S(2)}, u32[]{:S(2)}) collective-permute-start(bf16[360,1280]{1,0:T(8,128)(2,1)} %get-tuple-element.5), channel_id=1, source_target_pairs={{0,16},{8,24},{16,0},{24,8},{1,17},{9,25},{17,1},{25,9},{2,18},{10... | collective-permute-start | bytes 2764808 | tf_op jit(solution)/shard_map/ppermute | solution.py:524
  71.5 28.0 %copy-start.2 = (f32[360,1280]{1,0:T(8,128)S(1)}, f32[360,1280]{1,0:T(8,128)}, u32[]{:S(2)}) copy-start(f32[360,1280]{1,0:T(8,128)} %get-tuple-element.4) | copy-start | bytes 5529604
where the time goes:
time: 102 us
  Pallas kernels  94.7 us (93%)
  local copies, waits for them, and re-layouts  2.91 us (3%)
  other arithmetic  2.56 us (3%)
  starting transfers between devices  1.19 us (1%)
    pallas_call x1, Pallas kernels, rhs_call(): pl.pallas_call(functools.partial(rhs_kernel, height, stride, width, group...  41.9 us
    pallas_call x1, Pallas kernels, gram_call(): pl.pallas_call(functools.partial(gram_kernel, height, stride, width, grou...  28 us
    pallas_call x1, Pallas kernels, gather_call(): pl.pallas_call(gather_kernel, in_specs=[pl.BlockSpec(memory_space=pltpu.V...  24.9 us
    unnamed x8, local copies, waits for them, and re-layouts  2.64 us
    add x1, other arithmetic, body(): return (gram, keep + back.astype(jnp.float32))  2.56 us
  transfers between devices with their start and end apart: 1, of which 0 were waited for; matrix products, arithmetic and copies ran while one was open for 1% of the time, Pallas kernels for 27%

commit v1 on v0

v1 whole, which is shorter than its diff:
```python
import functools

import jax
import jax.numpy as jnp
from jax import lax
from jax.experimental import pallas as pl
from jax.experimental.pallas import tpu as pltpu
from jax.sharding import PartitionSpec as P

keep_off = 0.9
LANES = 128
KCHUNKS = 8


MESH = pl.DeviceIdType.MESH


def expand(base_of, live, channels, scratch, height, stride, width):
    pixels = live.shape[1]
    lane = lax.broadcasted_iota(jnp.int32, (1, pixels), 1)
    col = lane % width
    row = (lane // stride) % height

    def shifted(value, step, inside):
        return jnp.where(inside, pltpu.roll(value, (-step) % pixels, 1), 0.0)

    for first in range(0, channels, 16):
        size = min(16, channels - first)
        base = jnp.where(live > 0.0, base_of(first, size), 0.0)
        for b in range(3):
            if b == 1:
                across = base
            else:
                across = shifted(base, b - 1, (col + (b - 1) >= 0) & (col + (b - 1) < width))
            for a in range(3):
                if a == 1:
                    both = across
                else:
                    both = shifted(across, (a - 1) * stride, (row + (a - 1) >= 0) & (row + (a - 1) < height))
                for chunk in range(pixels // LANES):
                    scratch[chunk, pl.ds(first * 9 + 3 * a + b, size, stride=9), :] = both[
                        :, chunk * LANES : (chunk + 1) * LANES
                    ]


def spread(rows_of, live, channels, scratch, chunks, first_chunk, width):
    col = lax.broadcasted_iota(jnp.int32, (1, LANES), 1) % width
    held = scratch.shape[0]
    for h in range(max(first_chunk - 1, 0), min(first_chunk + held + 1, chunks)):
        value = rows_of(h)
        for first in range(0, channels, 8):
            size = min(8, channels - first)
            base = jnp.where(live > 0.0, value[first : first + size], 0.0)
            for b in range(3):
                if b == 1:
                    across = base
                else:
                    inside = (col + (b - 1) >= 0) & (col + (b - 1) < width)
                    across = jnp.where(inside, pltpu.roll(base, (1 - b) % LANES, 1), 0.0)
                for a in range(3):
                    to = h + 1 - a - first_chunk
                    if 0 <= to < held:
                        scratch[to, pl.ds(first * 9 + 3 * a + b, size, stride=9), :] = across
    for edge, a in ((0, 0), (chunks - 1, 2)):
        to = edge - first_chunk
        if 0 <= to < held:
            for first in range(0, channels, 8):
                size = min(8, channels - first)
                for b in range(3):
                    scratch[to, pl.ds(first * 9 + 3 * a + b, size, stride=9), :] = jnp.zeros(
                        (size, LANES), jnp.float32
                    )


def client_lanes(count_ref, first, clients, client, slot, total):
    count = jnp.zeros(client.shape, jnp.int32)
    for index in range(clients):
        count = jnp.where(client == index, count_ref[first + index], count)
    live = jnp.where(slot < count, 1.0, 0.0)
    return live, 1.0 / (total * count.astype(jnp.float32))


def step_kernel(
    groups, slots, width, count_ref, x_ref, w_ref, gram_ref, rhs_ref,
    xall, tsend, trecv, flat, wbuf, tall_wide, patch, scaled, across, square,
    part_ref, ybuf, sums, zbuf, obuf, rbuf, abuf, cbuf, vbuf, ubuf, wide, narrow, mine_ref,
    tss, tsr, hs, hr, ws, ys, yr, zs, zr, gs, gr, fs, fr, cs, cr, vs, vr,
):
    blks, clients, stride, channels = xall.shape
    height = blks
    pieces, depth = part_ref.shape[:2]
    cols = part_ref.shape[4]
    tile = trecv.shape[2]
    tall = tall_wide.shape[1]
    pixels = height * stride
    image = slots * width
    mine = rhs_ref.shape[0]
    total = count_ref.shape[0] * height * width
    client, blk = lax.axis_index("client"), lax.axis_index("blk")
    z, y = blk // 2, blk % 2
    core, side = client % 2, client // 2
    other = 1 - y
    core_mate = client + 1 - 2 * core
    x_mate = (client + 2) % clients
    core_dev, x_dev, y_dev = (core_mate, blk), (x_mate, blk), (client, blk + 1 - 2 * y)
    up_dev, down_dev = (client, blk + 2), (client, blk - 2)

    def level(d):
        return (z + d) % depth

    def z_dev(d):
        return (client, level(d) * 2 + y)

    def near(d):
        return (blk + d) % blks

    def w_copy(q):
        return pltpu.make_async_copy(w_ref.at[:, :, pl.ds(q * cols, cols)], wbuf.at[q], ws.at[q])

    for q in range(pieces):
        w_copy(q).start()

    barrier = pltpu.get_barrier_semaphore()
    for device in [core_dev, x_dev] + [(client, near(d)) for d in range(1, blks)]:
        pl.semaphore_signal(barrier, inc=1, device_id=device, device_id_type=MESH)
    for b in range(blks):
        tsend[b] = x_ref[:, b * tile : (b + 1) * tile]
    xall[blk, client] = x_ref[...]
    pl.semaphore_wait(barrier, blks + 1)

    def send(src, dst, send_sem, recv_sem, device):
        return pltpu.make_async_remote_copy(
            src_ref=src, dst_ref=dst, send_sem=send_sem, recv_sem=recv_sem, device_id=device, device_id_type=MESH
        )

    def tile_copy(d):
        return send(tsend.at[near(d)], trecv.at[blk], tss.at[d], tsr.at[blk], (client, near(d)))

    def tile_arrival(d):
        here = trecv.at[near(d)]
        return send(here, here, tss.at[d], tsr.at[near(d)], (client, near(d)))

    def hop(lane, c, b, device, own=False):
        dst = xall.at[b, c]
        src = x_ref if own else dst
        return send(src, dst, hs.at[lane, c * blks + b], hr.at[c * blks + b], device)

    def relay(d, mate, act, arrive=True):
        own = d == 0 and not mate

        def forward_block():
            b = (z + d) * 2 + (other if mate else y)
            if arrive and not own:
                hop(0, client, b, core_dev).wait_recv()
            if own:
                act(hop(3, client, b, y_dev, own))
            if d <= 0:
                pl.when(z + 1 < depth)(lambda: act(hop(0, client, b, up_dev, own)))
            if d >= 0:
                pl.when(z > 0)(lambda: act(hop(1, client, b, down_dev, own)))
            act(hop(2, client, b, x_dev, own))
            act(hop(4, client, b, core_dev, own))

        if d == 0:
            forward_block()
        else:
            pl.when((z + d >= 0) & (z + d < depth))(forward_block)

    def hand_over(b, act, arrive=True):
        if arrive:
            hop(2, x_mate, b, core_dev).wait_recv()
        act(hop(4, x_mate, b, core_dev))

    def start(copy):
        copy.start()

    def wait_send(copy):
        copy.wait_send()

    line = [(0, False), (0, True)]
    for distance in range(1, depth):
        line += [(-distance, False), (distance, False), (-distance, True), (distance, True)]

    for d in range(1, blks):
        tile_copy(d).start()
    relay(0, False, start)

    def y_copy(q):
        return send(part_ref.at[q, :, other], ybuf.at[q], ys.at[q], yr.at[q], y_dev)

    def z_copy(q, d):
        return send(sums.at[q, level(d)], zbuf.at[q, d], zs.at[q, d], zr.at[q, d], z_dev(d))

    def share(q, d, to):
        here = obuf.at[q, level(d), y]
        return send(here, here, gs.at[q, to], gr.at[q, to], z_dev(to))

    def forward(q, d, column):
        here = obuf.at[q, level(d), column]
        return send(here, here, fs.at[q, d], fr.at[q, level(d)], y_dev)

    def core_copy(q):
        return send(abuf.at[q], cbuf.at[q], cs.at[q], cr.at[q], core_dev)

    def x_copy(q):
        return send(vbuf.at[q], ubuf.at[q], vs.at[q], vr.at[q], x_dev)

    lane = lax.broadcasted_iota(jnp.int32, (1, pixels), 1)
    who = (lane // image) % groups
    live, scale = client_lanes(count_ref, client * groups, groups, who, (lane // width) % slots, total)

    def patches():
        trecv[blk] = tsend[blk]
        for d in range(1, blks):
            tile_arrival(d).wait_recv()
        flat[...] = trecv[...].reshape(pixels, tile).astype(jnp.float32).T
        expand(lambda first, size: flat[first : first + size, :], live, tile, tall_wide, height, stride, width)
        for chunk in range(tall_wide.shape[0]):
            span = slice(chunk * LANES, (chunk + 1) * LANES)
            value = tall_wide[chunk]
            patch[:, span] = value.astype(jnp.bfloat16)
            scaled[:, span] = (value * scale[:, span]).astype(jnp.bfloat16)
        flipped = patch[...].T
        for h in range(height):
            for group in range(groups):
                across[group, h * image : (h + 1) * image] = flipped[
                    (h * groups + group) * image : (h * groups + group + 1) * image
                ]

    def multiply(q):
        w_copy(q).wait()
        for group in range(groups):
            term = jnp.dot(across[group], wbuf[q, group], preferred_element_type=jnp.float32)
            for h in range(height):
                part_ref[q, h // 2, h % 2, group * image : (group + 1) * image] = term[h * image : (h + 1) * image]
        y_copy(q).start()

    def damping():
        for group in range(groups):
            term = jnp.zeros((tall, 1), jnp.float32)
            for chunk in range(tall_wide.shape[0]):
                span = slice(chunk * LANES, (chunk + 1) * LANES)
                value = tall_wide[chunk]
                value = jnp.where(who[:, span] == group, value * value * scale[:, span], 0.0)
                term += jnp.sum(value, axis=1, keepdims=True)
            square[group] = term * (1.0 - keep_off)

    def damp(q):
        total = None
        for group in range(groups):
            term = square[group] * wbuf[q, group].astype(jnp.float32)
            total = term if total is None else total + term
        rbuf[q] = total

    def add_y(q):
        y_copy(q).wait_recv()
        for d in range(depth):
            sums[q, level(d)] = part_ref[q, level(d), y] + ybuf[q, level(d)]
        for d in range(1, depth):
            z_copy(q, d).start()

    def add_z(q):
        total = sums[q, z]
        for d in range(1, depth):
            z_copy(q, d).wait_recv()
            total = total + zbuf[q, d]
        obuf[q, z, y] = total.astype(jnp.bfloat16)
        for d in range(1, depth):
            share(q, 0, d).start()
        forward(q, 0, y).start()

    def pass_on(q):
        for d in range(1, depth):
            share(q, depth - d, d).wait_recv()
            forward(q, depth - d, y).start()

    def rows_of(q, holder):
        if mine % 8 == 0:
            return rbuf[q, pl.ds(pl.multiple_of(holder * mine, 8), mine), :]
        value = rbuf[q, :mine, :]
        for index in range(1, tall // mine):
            value = jnp.where(holder == index, rbuf[q, index * mine : (index + 1) * mine, :], value)
        return value

    def cross(q):
        for d in range(depth):
            forward(q, d, other).wait_recv()
        product = jnp.dot(scaled[...], obuf[q].reshape(pixels, cols), preferred_element_type=jnp.float32)
        rbuf[q] = rbuf[q] + keep_off * product
        for far in range(2):
            abuf[q, far] = rows_of(q, far * 2 + 1 - core).astype(jnp.bfloat16)
        core_copy(q).start()

    def finish(q):
        core_copy(q).wait_recv()
        far = 1 - side
        away = rows_of(q, far * 2 + core) + cbuf[q, far].astype(jnp.float32)
        vbuf[q] = away.astype(jnp.bfloat16)
        x_copy(q).start()
        span = slice(q * cols, (q + 1) * cols)
        rhs_ref[:, span] = rows_of(q, client) + cbuf[q, side].astype(jnp.float32)

    def settle(q):
        x_copy(q).wait_recv()
        span = slice(q * cols, (q + 1) * cols)
        rhs_ref[:, span] = rhs_ref[:, span] + ubuf[q].astype(jnp.float32)

    def tick(step):
        if step < pieces:
            add_y(step)
        if 0 <= step - 1 < pieces:
            add_z(step - 1)
        if step < pieces:
            damp(step)
        if 0 <= step - 2 < pieces:
            pass_on(step - 2)
        if 0 <= step - 3 < pieces:
            cross(step - 3)
        if 0 <= step - 4 < pieces:
            finish(step - 4)

    patches()
    later = line[1:]
    for q in range(pieces):
        for entry in later[:2]:
            relay(*entry, start)
        later = later[2:]
        multiply(q)
    damping()
    for entry in later:
        relay(*entry, start)
    crossing = [(z + d) % depth * 2 + p for d in range(depth) for p in (0, 1)]
    before = 3
    each = -(-len(crossing) // before)
    for step in range(before):
        tick(step)
        for b in crossing[step * each : (step + 1) * each]:
            hand_over(b, start)
    far_mate = (core_mate + 2) % clients
    for b in range(blks):
        for c in (core_mate, far_mate):
            hop(4, c, b, core_dev).wait_recv()

    own = blk * tile + client * (mine // 9)
    span = lax.broadcasted_iota(jnp.int32, (1, LANES), 1)
    all_live, all_scale = client_lanes(
        count_ref, 0, count_ref.shape[0], span // image, (span // width) % slots, total
    )
    held = wide.shape[0]
    passes = [first for first in range(0, height, held)]

    def block_rows(h, lanes):
        return xall[h, :, :, lanes].reshape(LANES, -1)

    chosen = (
        lax.broadcasted_iota(jnp.int32, (mine // 9, channels), 1)
        == lax.broadcasted_iota(jnp.int32, (mine // 9, channels), 0) + own
    )
    chosen = jnp.where(chosen, 1.0, 0.0).astype(jnp.bfloat16)

    def own_rows(h):
        return lax.dot_general(
            chosen, block_rows(h, slice(None)), (((1,), (1,)), ((), ())), preferred_element_type=jnp.float32
        )

    for first in passes:
        spread(own_rows, all_live, mine // 9, wide, height, first, width)
        for chunk in range(held):
            mine_ref[:, (first + chunk) * LANES : (first + chunk + 1) * LANES] = (
                wide[chunk, :mine] * all_scale
            ).astype(jnp.bfloat16)

    tiles = gram_ref.shape[0]
    events = {}
    for index, step in enumerate(range(before, pieces + 4)):
        events.setdefault(min(index, tiles - 1), []).append(functools.partial(tick, step))

    def gram_tile(t, carry):
        for when, actions in events.items():

            @pl.when(t == when)
            def _():
                for action in actions:
                    action()

        lanes = pl.ds(pl.multiple_of(t * LANES, LANES), LANES)
        for first in passes:
            spread(
                lambda h: block_rows(h, lanes).astype(jnp.float32).T, all_live, LANES, wide, height, first, width
            )
            for chunk in range(held):
                narrow[:, chunk * LANES : (chunk + 1) * LANES] = wide[chunk].astype(jnp.bfloat16)
            product = lax.dot_general(
                mine_ref[:, first * LANES : (first + held) * LANES], narrow[...],
                (((1,), (1,)), ((), ())), preferred_element_type=jnp.float32,
            )
            if first != 0:
                product = product + gram_ref[t]
            if first == passes[-1]:
                where_diag = own * 9 - t * product.shape[1]
                on_diag = (
                    lax.broadcasted_iota(jnp.int32, product.shape, 1)
                    == lax.broadcasted_iota(jnp.int32, product.shape, 0) + where_diag
                )
                product = jnp.where(on_diag, product, keep_off * product)
            gram_ref[t] = product
        return carry

    lax.fori_loop(0, tiles, gram_tile, 0)

    for q in range(pieces):
        settle(q)
    for entry in line:
        relay(*entry, wait_send, False)
    for b in crossing:
        hand_over(b, wait_send, False)
    for d in range(1, blks):
        tile_copy(d).wait_send()
    for q in range(pieces):
        y_copy(q).wait_send()
        core_copy(q).wait_send()
        x_copy(q).wait_send()
        for d in range(1, depth):
            z_copy(q, d).wait_send()
            share(q, 0, d).wait_send()
        for d in range(depth):
            forward(q, d, y).wait_send()


def step_call(counts, x, weights, clients, blks, slots, width):
    stride, channels = x.shape
    groups, tall, columns = weights.shape
    mine = tall // clients
    tile = tall // 9
    height = blks
    pixels = height * stride
    everyone = clients * stride
    pieces = columns // 256 if columns % 256 == 0 else 1
    cols = columns // pieces
    depth = blks // 2
    held = min(KCHUNKS, height)
    sem = pltpu.SemaphoreType.DMA
    f32, bf16 = jnp.float32, jnp.bfloat16
    hop = pltpu.VMEM((pieces, depth, stride, cols), f32)
    return pl.pallas_call(
        functools.partial(step_kernel, groups, slots, width),
        in_specs=[
            pl.BlockSpec(memory_space=pltpu.SMEM),
            pl.BlockSpec(memory_space=pltpu.VMEM),
            pl.BlockSpec(memory_space=pltpu.HBM),
        ],
        out_specs=[pl.BlockSpec(memory_space=pltpu.VMEM)] * 2,
        out_shape=[
            pltpu.VMEM((channels // LANES, mine, LANES * 9), f32),
            pltpu.VMEM((mine, columns), f32),
        ],
        scratch_shapes=[
            pltpu.VMEM((blks, clients, stride, channels), bf16),
            pltpu.VMEM((blks, stride, tile), bf16),
            pltpu.VMEM((blks, stride, tile), bf16),
            pltpu.VMEM((tile, pixels), f32),
            pltpu.VMEM((pieces, groups, tall, cols), bf16),
            pltpu.VMEM((pixels // LANES, tall, LANES), f32),
            pltpu.VMEM((tall, pixels), bf16),
            pltpu.VMEM((tall, pixels), bf16),
            pltpu.VMEM((groups, pixels // groups, tall), bf16),
            pltpu.VMEM((groups, tall, 1), f32),
            pltpu.VMEM((pieces, depth, 2, stride, cols), f32),
            hop,
            hop,
            hop,
            pltpu.VMEM((pieces, depth, 2, stride, cols), bf16),
            pltpu.VMEM((pieces, tall, cols), f32),
            pltpu.VMEM((pieces, 2, mine, cols), bf16),
            pltpu.VMEM((pieces, 2, mine, cols), bf16),
            pltpu.VMEM((pieces, mine, cols), bf16),
            pltpu.VMEM((pieces, mine, cols), bf16),
            pltpu.VMEM((held, LANES * 9, LANES), f32),
            pltpu.VMEM((LANES * 9, held * LANES), bf16),
            pltpu.VMEM((mine, height * LANES), bf16),
            sem((blks,)),
            sem((blks,)),
            sem((5, clients * blks)),
            sem((clients * blks,)),
            sem((pieces,)),
            sem((pieces,)),
            sem((pieces,)),
        ]
        + [sem((pieces, depth))] * 6
        + [sem((pieces,))] * 4,
        compiler_params=pltpu.CompilerParams(
            collective_id=1, has_side_effects=True, vmem_limit_bytes=VMEM_MIB * 1024 * 1024
        ),
    )(counts, x, weights)


VMEM_MIB = 44


def store_kernel(gram_tiles, rhs_ref, gram_ref, out_ref, sems):
    tiles, rows, wide = gram_tiles.shape

    def tile_copy(t):
        return pltpu.make_async_copy(gram_tiles.at[t], gram_ref.at[:, pl.ds(t * wide, wide)], sems.at[t])

    rhs_copy = pltpu.make_async_copy(rhs_ref, out_ref, sems.at[tiles])
    for t in range(tiles):
        tile_copy(t).start()
    rhs_copy.start()
    for t in range(tiles):
        tile_copy(t).wait()
    rhs_copy.wait()


def store_call(gram_tiles, rhs):
    tiles, rows, wide = gram_tiles.shape
    return pl.pallas_call(
        store_kernel,
        in_specs=[pl.BlockSpec(memory_space=pltpu.VMEM)] * 2,
        out_specs=[pl.BlockSpec(memory_space=pl.ANY)] * 2,
        out_shape=[
            jax.ShapeDtypeStruct((rows, tiles * wide), jnp.float32),
            jax.ShapeDtypeStruct(rhs.shape, jnp.float32),
        ],
        scratch_shapes=[pltpu.SemaphoreType.DMA((tiles + 1,))],
        compiler_params=pltpu.CompilerParams(vmem_limit_bytes=24 * 1024 * 1024),
    )(gram_tiles, rhs)


def body(activations, sample_count, client_weights):
    blk_count = lax.axis_size("blk")
    group_size, slot_count, rows_here, width, channels = activations.shape
    client_groups = sample_count.shape[0] // group_size
    assert rows_here == 1 and client_groups * group_size * slot_count * width == LANES
    shard = activations.transpose(2, 0, 1, 3, 4).reshape(group_size * slot_count * width, channels)
    gram_tiles, rhs = step_call(
        sample_count, shard, client_weights, client_groups, blk_count, slot_count, width
    )
    return tuple(store_call(gram_tiles, rhs))


def solution(mesh):
    in_specs = (P("client", None, "blk", None, None), P(), P("client", "blk", None))
    out_specs = (P(("blk", "client"), None), P(("blk", "client"), None))
    return jax.shard_map(body, mesh=mesh, in_specs=in_specs, out_specs=out_specs, check_vma=False)
```

time: 102 us -> 74.9 us (0.73)
  Pallas kernels: 94.7 us -> 74.1 us
  local copies, waits for them, and re-layouts: 2.91 us -> 0 us
  other arithmetic: 2.56 us -> 0 us
  starting transfers between devices: 1.19 us -> 0 us
    pallas_call x3 -> x2, Pallas kernels: 94.7 us -> 74.1 us  [the longest x1 67.6 us: step_call(): pl.pallas_call(functools.partial(step_kernel, groups, slots, width), in_s...]
    unnamed x8 -> x0, local copies, waits for them, and re-layouts: 2.64 us -> none
    add x1 -> x0, other arithmetic: 2.56 us -> none  [body(): return (gram, keep + back.astype(jnp.float32))]
    ppermute x1 -> x0, starting transfers between devices: 1.19 us -> none  [body(): lax.ppermute(away, 'client', [(c, (c + 2) % client_groups) for c in range...]
  transfers between devices with their start and end apart: 1 -> 0, of which waited for: 0 -> 0; matrix products, arithmetic and copies ran while one was open for 1% -> 0% of each run, Pallas kernels for 27% -> 0%
where the time goes in v1:
time: 74.9 us; the launch traced here: 74.7 us
  Pallas kernels  74.1 us (99%)
    pallas_call x1, Pallas kernels, step_call(): pl.pallas_call(functools.partial(step_kernel, groups, slots, width), in_s...  67.6 us
    pallas_call x1, Pallas kernels, store_call(): pl.pallas_call(store_kernel, in_specs=[pl.BlockSpec(memory_space=pltpu.VM...  6.46 us

profile of v1, /device:TPU:0, one launch (start us, length us, event | category | flops | bytes accessed | tf_op | source)
XLA Modules:
  0.0 74.7 jit_solution(10686744267896622701)
XLA Ops:
  0.6 67.6 %shard_map.50 = (f32[10,360,1152]{2,1,0:T(8,128)S(1)}, f32[360,1280]{1,0:T(8,128)S(1)}) custom-call(s32[8]{0:T(128)} %count_ref.1, bf16[32,1280]{1,0:T(8,128)(2,1)} %bitcast.1, bf16[2,1440,1280]{2,1,0:T(8,128)(2,1)} %w_ref.1), custom_call_target="tpu_custom_call" | custom-call | tf_op jit(solution)/shard_map/pallas_call | solution.py:445
  68.3 6.5 %shard_map.51 = (f32[360,11520]{1,0:T(8,128)}, f32[360,1280]{1,0:T(8,128)}) custom-call(f32[10,360,1152]{2,1,0:T(8,128)S(1)} %get-tuple-element.4.gram_tiles, f32[360,1280]{1,0:T(8,128)S(1)} %get-tuple-element.5.rhs_ref), custom_call_target="tpu_custom_call" | custom-call | tf_op jit(solution)/shard_map/pallas_call | solution.py:517

commit v2 on v1

--- a/solution.py
+++ b/solution.py
@@ -72,6 +72,39 @@
                     )
 
 
+START, GRAM, TILE, OVER = 12.5, 27.0, 1.9, 1.1
+PIECE = 256
+
+
+def plan(pieces, depth, part, tiles):
+    listed = [(START + 0.46 * part * pieces, "damping")]
+    for q in range(pieces):
+        at = START + 0.45 * part * q
+        listed.append((at, "multiply", q))
+        listed.append((START + 0.47 * part * pieces + 0.5 * part * q, "damp", q))
+        at = START + 1.5 + 2.8 * part * (q + 1)
+        listed.append((at, "add_y", q))
+        for name, wait in (
+            ("add_z", 2.8 * part + 2.5), ("pass_on", 1.4 * part + 2.5),
+            ("cross", 1.4 * part + 1.5), ("finish", 0.8 * part + 1.7),
+        ):
+            at += wait
+            listed.append((at, name, q))
+    for index in range(4 * depth - 2):
+        distance = (index + 2) // 4
+        at = START - 1.0 + 2.2 * (distance - 1) + 1.5 * (index % 4 in (0, 1) if distance else index)
+        if index > 3:
+            listed.append((at, "relay", index))
+        listed.append((max(at + 3.0, START - 0.5 + OVER * index), "over", index))
+    listed.sort(key=lambda entry: entry[0])
+    before = [entry[1:] for entry in listed if entry[0] < GRAM or entry[1] in ("relay", "over")]
+    during = [[] for _ in range(tiles + 1)]
+    for at, *entry in listed:
+        if tuple(entry) not in before:
+            during[min(int((at - GRAM) / TILE), tiles)].append(tuple(entry))
+    return before, during
+
+
 def client_lanes(count_ref, first, clients, client, slot, total):
     count = jnp.zeros(client.shape, jnp.int32)
     for index in range(clients):
@@ -83,7 +116,7 @@
 def step_kernel(
     groups, slots, width, count_ref, x_ref, w_ref, gram_ref, rhs_ref,
     xall, tsend, trecv, flat, wbuf, tall_wide, patch, scaled, across, square,
-    part_ref, ybuf, sums, zbuf, obuf, rbuf, abuf, cbuf, vbuf, ubuf, wide, narrow, mine_ref,
+    part_ref, ybuf, sums, zbuf, obuf, rbuf, abuf, cbuf, vbuf, ubuf, wide, narrow, narrow_next, mine_ref,
     tss, tsr, hs, hr, ws, ys, yr, zs, zr, gs, gr, fs, fr, cs, cr, vs, vr,
 ):
     blks, clients, stride, channels = xall.shape
@@ -166,10 +199,17 @@
         else:
             pl.when((z + d >= 0) & (z + d < depth))(forward_block)
 
-    def hand_over(b, act, arrive=True):
-        if arrive:
-            hop(2, x_mate, b, core_dev).wait_recv()
-        act(hop(4, x_mate, b, core_dev))
+    def hand_over(d, mate, act, arrive=True):
+        def pass_block():
+            b = (z + d) * 2 + (other if mate else y)
+            if arrive:
+                hop(2, x_mate, b, core_dev).wait_recv()
+            act(hop(4, x_mate, b, core_dev))
+
+        if d == 0:
+            pass_block()
+        else:
+            pl.when((z + d >= 0) & (z + d < depth))(pass_block)
 
     def start(copy):
         copy.start()
@@ -213,6 +253,8 @@
         trecv[blk] = tsend[blk]
         for d in range(1, blks):
             tile_arrival(d).wait_recv()
+        for index in range(1, 4):
+            relay(*line[index], start)
         flat[...] = trecv[...].reshape(pixels, tile).astype(jnp.float32).T
         expand(lambda first, size: flat[first : first + size, :], live, tile, tall_wide, height, stride, width)
         for chunk in range(tall_wide.shape[0]):
@@ -243,14 +285,22 @@
                 value = tall_wide[chunk]
                 value = jnp.where(who[:, span] == group, value * value * scale[:, span], 0.0)
                 term += jnp.sum(value, axis=1, keepdims=True)
-            square[group] = term * (1.0 - keep_off)
+            square[group] = jnp.broadcast_to(term * (1.0 - keep_off), (tall, LANES))
 
     def damp(q):
-        total = None
-        for group in range(groups):
-            term = square[group] * wbuf[q, group].astype(jnp.float32)
-            total = term if total is None else total + term
-        rbuf[q] = total
+        rows = 80 if tall % 80 == 0 else tall
+
+        def block(index, carry):
+            span = pl.ds(pl.multiple_of(index * rows, 8), rows)
+            for first in range(0, cols, LANES):
+                total = None
+                for group in range(groups):
+                    term = square[group, span, :] * wbuf[q, group, span, first : first + LANES].astype(jnp.float32)
+                    total = term if total is None else total + term
+                rbuf[q, span, first : first + LANES] = total
+            return carry
+
+        lax.fori_loop(0, tall // rows, block, 0)
 
     def add_y(q):
         y_copy(q).wait_recv()
@@ -305,37 +355,26 @@
         span = slice(q * cols, (q + 1) * cols)
         rhs_ref[:, span] = rhs_ref[:, span] + ubuf[q].astype(jnp.float32)
 
-    def tick(step):
-        if step < pieces:
-            add_y(step)
-        if 0 <= step - 1 < pieces:
-            add_z(step - 1)
-        if step < pieces:
-            damp(step)
-        if 0 <= step - 2 < pieces:
-            pass_on(step - 2)
-        if 0 <= step - 3 < pieces:
-            cross(step - 3)
-        if 0 <= step - 4 < pieces:
-            finish(step - 4)
-
+    actions = {
+        "multiply": multiply,
+        "damping": damping,
+        "damp": damp,
+        "add_y": add_y,
+        "add_z": add_z,
+        "pass_on": pass_on,
+        "cross": cross,
+        "finish": finish,
+        "relay": lambda index: relay(*line[index], start),
+        "over": lambda index: hand_over(*line[index], start),
+    }
+
+    def run(listed):
+        for name, *values in listed:
+            actions[name](*values)
+
+    before, during = plan(pieces, depth, cols / 256, gram_ref.shape[0])
     patches()
-    later = line[1:]
-    for q in range(pieces):
-        for entry in later[:2]:
-            relay(*entry, start)
-        later = later[2:]
-        multiply(q)
-    damping()
-    for entry in later:
-        relay(*entry, start)
-    crossing = [(z + d) % depth * 2 + p for d in range(depth) for p in (0, 1)]
-    before = 3
-    each = -(-len(crossing) // before)
-    for step in range(before):
-        tick(step)
-        for b in crossing[step * each : (step + 1) * each]:
-            hand_over(b, start)
+    run(before)
     far_mate = (core_mate + 2) % clients
     for b in range(blks):
         for c in (core_mate, far_mate):
@@ -371,49 +410,66 @@
             ).astype(jnp.bfloat16)
 
     tiles = gram_ref.shape[0]
-    events = {}
-    for index, step in enumerate(range(before, pieces + 4)):
-        events.setdefault(min(index, tiles - 1), []).append(functools.partial(tick, step))
-
-    def gram_tile(t, carry):
-        for when, actions in events.items():
-
-            @pl.when(t == when)
-            def _():
-                for action in actions:
-                    action()
-
+
+    def fill(t, first, kept):
         lanes = pl.ds(pl.multiple_of(t * LANES, LANES), LANES)
-        for first in passes:
-            spread(
-                lambda h: block_rows(h, lanes).astype(jnp.float32).T, all_live, LANES, wide, height, first, width
+        spread(lambda h: block_rows(h, lanes).astype(jnp.float32).T, all_live, LANES, wide, height, first, width)
+        for chunk in range(held):
+            kept[:, chunk * LANES : (chunk + 1) * LANES] = wide[chunk].astype(jnp.bfloat16)
+
+    def product_of(t, first, kept):
+        product = lax.dot_general(
+            mine_ref[:, first * LANES : (first + held) * LANES], kept[...],
+            (((1,), (1,)), ((), ())), preferred_element_type=jnp.float32,
+        )
+        if first != 0:
+            product = product + gram_ref[t]
+        if first == passes[-1]:
+            where_diag = own * 9 - t * product.shape[1]
+            on_diag = (
+                lax.broadcasted_iota(jnp.int32, product.shape, 1)
+                == lax.broadcasted_iota(jnp.int32, product.shape, 0) + where_diag
             )
-            for chunk in range(held):
-                narrow[:, chunk * LANES : (chunk + 1) * LANES] = wide[chunk].astype(jnp.bfloat16)
-            product = lax.dot_general(
-                mine_ref[:, first * LANES : (first + held) * LANES], narrow[...],
-                (((1,), (1,)), ((), ())), preferred_element_type=jnp.float32,
-            )
-            if first != 0:
-                product = product + gram_ref[t]
-            if first == passes[-1]:
-                where_diag = own * 9 - t * product.shape[1]
-                on_diag = (
-                    lax.broadcasted_iota(jnp.int32, product.shape, 1)
-                    == lax.broadcasted_iota(jnp.int32, product.shape, 0) + where_diag
-                )
-                product = jnp.where(on_diag, product, keep_off * product)
-            gram_ref[t] = product
-        return carry
-
-    lax.fori_loop(0, tiles, gram_tile, 0)
-
+            product = jnp.where(on_diag, product, keep_off * product)
+        gram_ref[t] = product
+
+    def happen(t, options):
+        for when in options:
+            if during[when]:
+                pl.when(t == when)(functools.partial(run, during[when]))
+
+    if len(passes) == 1 and tiles % 2 == 0:
+        fill(0, 0, narrow)
+
+        def pair(index, carry):
+            t = index * 2
+            happen(t, range(0, tiles, 2))
+            product_of(t, 0, narrow)
+            fill(t + 1, 0, narrow_next)
+            happen(t + 1, range(1, tiles, 2))
+            product_of(t + 1, 0, narrow_next)
+            fill(jnp.minimum(t + 2, tiles - 1), 0, narrow)
+            return carry
+
+        lax.fori_loop(0, tiles // 2, pair, 0)
+    else:
+
+        def single(t, carry):
+            happen(t, range(tiles))
+            for first in passes:
+                fill(t, first, narrow)
+                product_of(t, first, narrow)
+            return carry
+
+        lax.fori_loop(0, tiles, single, 0)
+
+    run(during[tiles])
     for q in range(pieces):
         settle(q)
     for entry in line:
         relay(*entry, wait_send, False)
-    for b in crossing:
-        hand_over(b, wait_send, False)
+    for entry in line:
+        hand_over(*entry, wait_send, False)
     for d in range(1, blks):
         tile_copy(d).wait_send()
     for q in range(pieces):
@@ -435,7 +491,7 @@
     height = blks
     pixels = height * stride
     everyone = clients * stride
-    pieces = columns // 256 if columns % 256 == 0 else 1
+    pieces = columns // PIECE if columns % PIECE == 0 else 1
     cols = columns // pieces
     depth = blks // 2
     held = min(KCHUNKS, height)
@@ -464,7 +520,7 @@
             pltpu.VMEM((tall, pixels), bf16),
             pltpu.VMEM((tall, pixels), bf16),
             pltpu.VMEM((groups, pixels // groups, tall), bf16),
-            pltpu.VMEM((groups, tall, 1), f32),
+            pltpu.VMEM((groups, tall, LANES), f32),
             pltpu.VMEM((pieces, depth, 2, stride, cols), f32),
             hop,
             hop,
@@ -477,6 +533,7 @@
             pltpu.VMEM((pieces, mine, cols), bf16),
             pltpu.VMEM((held, LANES * 9, LANES), f32),
             pltpu.VMEM((LANES * 9, held * LANES), bf16),
+            pltpu.VMEM((LANES * 9, held * LANES if height == held else LANES), bf16),
             pltpu.VMEM((mine, height * LANES), bf16),
             sem((blks,)),
             sem((blks,)),

time: 74.9 us -> 71.8 us (0.959)
  Pallas kernels: 74.1 us -> 71 us
    pallas_call x1, Pallas kernels: 67.6 us -> 64.6 us  [step_call(): pl.pallas_call(functools.partial(step_kernel, groups, slots, width), in_s...]
where the time goes in v2:
time: 71.8 us; the launch traced here: 71.7 us
  Pallas kernels  71 us (99%)
    pallas_call x1, Pallas kernels, step_call(): pl.pallas_call(functools.partial(step_kernel, groups, slots, width), in_s...  64.6 us
    pallas_call x1, Pallas kernels, store_call(): pl.pallas_call(store_kernel, in_specs=[pl.BlockSpec(memory_space=pltpu.VM...  6.46 us

profile of v2, /device:TPU:0, one launch (start us, length us, event | category | flops | bytes accessed | tf_op | source)
XLA Modules:
  0.0 71.7 jit_solution(7276781429593810690)
XLA Ops:
  0.6 64.6 %shard_map.50 = (f32[10,360,1152]{2,1,0:T(8,128)S(1)}, f32[360,1280]{1,0:T(8,128)S(1)}) custom-call(s32[8]{0:T(128)} %count_ref.1, bf16[32,1280]{1,0:T(8,128)(2,1)} %bitcast.1, bf16[2,1440,1280]{2,1,0:T(8,128)(2,1)} %w_ref.1), custom_call_target="tpu_custom_call" | custom-call | tf_op jit(solution)/shard_map/pallas_call | solution.py:501
  65.2 6.5 %shard_map.51 = (f32[360,11520]{1,0:T(8,128)}, f32[360,1280]{1,0:T(8,128)}) custom-call(f32[10,360,1152]{2,1,0:T(8,128)S(1)} %get-tuple-element.4.gram_tiles, f32[360,1280]{1,0:T(8,128)S(1)} %get-tuple-element.5.rhs_ref), custom_call_target="tpu_custom_call" | custom-call | tf_op jit(solution)/shard_map/pallas_call | solution.py:574

commit v3 on v2

--- a/solution.py
+++ b/solution.py
@@ -95,7 +95,8 @@
         at = START - 1.0 + 2.2 * (distance - 1) + 1.5 * (index % 4 in (0, 1) if distance else index)
         if index > 3:
             listed.append((at, "relay", index))
-        listed.append((max(at + 3.0, START - 0.5 + OVER * index), "over", index))
+        if index:
+            listed.append((max(at + 3.0, START - 0.5 + OVER * index), "over", index))
     listed.sort(key=lambda entry: entry[0])
     before = [entry[1:] for entry in listed if entry[0] < GRAM or entry[1] in ("relay", "over")]
     during = [[] for _ in range(tiles + 1)]
@@ -185,13 +186,14 @@
             b = (z + d) * 2 + (other if mate else y)
             if arrive and not own:
                 hop(0, client, b, core_dev).wait_recv()
+            if d != 0 or not mate:
+                act(hop(2, client, b, x_dev, own))
             if own:
                 act(hop(3, client, b, y_dev, own))
             if d <= 0:
                 pl.when(z + 1 < depth)(lambda: act(hop(0, client, b, up_dev, own)))
             if d >= 0:
                 pl.when(z > 0)(lambda: act(hop(1, client, b, down_dev, own)))
-            act(hop(2, client, b, x_dev, own))
             act(hop(4, client, b, core_dev, own))
 
         if d == 0:
@@ -204,6 +206,8 @@
             b = (z + d) * 2 + (other if mate else y)
             if arrive:
                 hop(2, x_mate, b, core_dev).wait_recv()
+            if d == 0 and not mate:
+                act(hop(3, x_mate, b, y_dev))
             act(hop(4, x_mate, b, core_dev))
 
         if d == 0:
@@ -255,6 +259,7 @@
             tile_arrival(d).wait_recv()
         for index in range(1, 4):
             relay(*line[index], start)
+        hand_over(*line[0], start)
         flat[...] = trecv[...].reshape(pixels, tile).astype(jnp.float32).T
         expand(lambda first, size: flat[first : first + size, :], live, tile, tall_wide, height, stride, width)
         for chunk in range(tall_wide.shape[0]):

time: 71.8 us -> 71.5 us (level)
  no operation moved by 1% of the time
where the time goes in v3:
time: 71.5 us; the launch traced here: 71.4 us
  Pallas kernels  70.7 us (99%)
    pallas_call x1, Pallas kernels, step_call(): pl.pallas_call(functools.partial(step_kernel, groups, slots, width), in_s...  64.3 us
    pallas_call x1, Pallas kernels, store_call(): pl.pallas_call(store_kernel, in_specs=[pl.BlockSpec(memory_space=pltpu.VM...  6.46 us

profile of v3, /device:TPU:0, one launch (start us, length us, event | category | flops | bytes accessed | tf_op | source)
XLA Modules:
  0.0 71.4 jit_solution(13519261607780656236)
XLA Ops:
  0.6 64.3 %shard_map.50 = (f32[10,360,1152]{2,1,0:T(8,128)S(1)}, f32[360,1280]{1,0:T(8,128)S(1)}) custom-call(s32[8]{0:T(128)} %count_ref.1, bf16[32,1280]{1,0:T(8,128)(2,1)} %bitcast.1, bf16[2,1440,1280]{2,1,0:T(8,128)(2,1)} %w_ref.1), custom_call_target="tpu_custom_call" | custom-call | tf_op jit(solution)/shard_map/pallas_call | solution.py:506
  64.9 6.5 %shard_map.51 = (f32[360,11520]{1,0:T(8,128)}, f32[360,1280]{1,0:T(8,128)}) custom-call(f32[10,360,1152]{2,1,0:T(8,128)S(1)} %get-tuple-element.4.gram_tiles, f32[360,1280]{1,0:T(8,128)S(1)} %get-tuple-element.5.rhs_ref), custom_call_target="tpu_custom_call" | custom-call | tf_op jit(solution)/shard_map/pallas_call | solution.py:579
